TPU v7x, 32 devices: a whole 2x2x4 slice. The times are simulated.
32 devices in a mesh: band: 2 (over x), grid: 16 (over z, y, core).
Axes of the slice: x: 2, y: 2, z: 4, core: 2. Of those that a mesh axis runs over, the one named last changes fastest.
Arguments:
- start_block: float32 [64, 128, 4, 128], P('band', 'grid'), may hold values from -6 to 6
- previous_block: float32 [64, 128, 4, 128], P('band', 'grid'), may hold values from -6 to 6
- previous_coupling: float32 [64, 64], replicated, may hold values from -0.75 to 0.75
- potential: float32 [128, 4, 128], P('grid'), may hold values from -2 to 2
- atom_cells: int32 [128, 128], P('grid'), may hold values from 0 to 7167, as said below
- atom_proj: float32 [128, 4, 128], P('grid'), may hold values from -1.08 to 1.08
- atom_strength: float32 [128, 4], P('grid'), may hold values from 0.5 to 4
- atom_count: int32 [16], P('grid'), may hold values from 1 to 8, as said below
Outputs:
- a_blocks: float32 [2, 64, 64], P(None, None, 'band')
- b_blocks: float32 [2, 64, 64], P(None, None, 'band')
- final_block: float32 [64, 128, 4, 128], P('band', 'grid')
Inputs may be any that keep to these rules, and one draw needn't show every extreme that they name: `atom_cells`: row a lists 128 distinct cells of atom a's sphere as row-major indices over (14) planes x 4 x 128, counted from the first plane of the slab that holds row a; indices of 4096 or more lie in the first 6 planes of the next slab; on the last slab every index is below 4096. `atom_count`: slots at or past a slab's count are not atoms.
All inputs are finite; a program needn't handle non-finite values.
Results may differ from a plain program's by a relative error of at most 0.0003.
Values sent between devices are 32-bit elements; how exact they have to be, the bound alone decides.
A program may use at most 64 MiB of HBM per device.

v0:
```python
import jax
import jax.numpy as jnp
from jax import lax
from jax.sharding import PartitionSpec as P

NB = 64
STEPS = 2
HIGHEST = lax.Precision.HIGHEST
STENCIL_WEIGHTS = (
    -5369.0 / 1800.0,
    12.0 / 7.0,
    -15.0 / 56.0,
    10.0 / 189.0,
    -1.0 / 112.0,
    2.0 / 1925.0,
    -1.0 / 16632.0,
)


def extended_2(block, sides, width):
    for axis, dim in sides:
        count = lax.axis_size(axis)
        forward = [(i, i + 1) for i in range(count - 1)]
        backward = [(target, source) for source, target in forward]
        low = lax.ppermute(
            lax.slice_in_dim(block, block.shape[dim] - width, None, axis=dim), axis, forward
        )
        high = lax.ppermute(lax.slice_in_dim(block, 0, width, axis=dim), axis, backward)
        block = jnp.concatenate([low, block, high], axis=dim)
    return block


def from_behind(block, axis, distance):
    devices = range(lax.axis_size(axis))
    route = [(i - distance, i) for i in devices if i - distance in devices]
    return lax.ppermute(block, axis, route)


def kinetic_local(haloed, planes):
    center = haloed[:, 6 : 6 + planes]
    width_y, width_z = (center.shape[2], center.shape[3])
    padded = jnp.pad(center, ((0, 0), (0, 0), (6, 6), (6, 6)))
    laplace = 3.0 * STENCIL_WEIGHTS[0] * center
    for k in range(1, 7):
        laplace = laplace + STENCIL_WEIGHTS[k] * (
            haloed[:, 6 + k : 6 + k + planes] + haloed[:, 6 - k : 6 - k + planes]
        )
        laplace = laplace + STENCIL_WEIGHTS[k] * (
            padded[:, :, 6 + k : 6 + k + width_y, 6 : 6 + width_z]
            + padded[:, :, 6 - k : 6 - k + width_y, 6 : 6 + width_z]
        )
        laplace = laplace + STENCIL_WEIGHTS[k] * (
            padded[:, :, 6 : 6 + width_y, 6 + k : 6 + k + width_z]
            + padded[:, :, 6 : 6 + width_y, 6 - k : 6 - k + width_z]
        )
    return -0.5 * laplace


def projector_terms(extended, atom_cells, atom_proj, atom_strength, live_count):
    states_dev = extended.shape[0]
    atom_slots, points = atom_cells.shape
    cell_list = atom_cells.reshape(-1)
    picked = jnp.take(extended, cell_list, axis=1).reshape(states_dev, atom_slots, points)
    coefficient = jnp.einsum("sap,ajp->saj", picked, atom_proj, precision=HIGHEST)
    live_mask = (jnp.arange(atom_slots, dtype=jnp.int32) < live_count).astype(jnp.float32)
    scaled = coefficient * (atom_strength * live_mask[:, None])[None]
    spread = jnp.einsum("saj,ajp->sap", scaled, atom_proj, precision=HIGHEST)
    return jnp.zeros_like(extended).at[:, cell_list].add(spread.reshape(states_dev, -1))


def factor_of(gram):
    factor = jnp.linalg.cholesky(gram)
    identity = jnp.eye(gram.shape[0], dtype=jnp.float32)
    inverse = jax.scipy.linalg.solve_triangular(factor, identity, lower=True)
    return (factor, inverse)


def shards(
    start_block,
    previous_block,
    previous_coupling,
    potential,
    atom_cells,
    atom_proj,
    atom_strength,
    atom_count,
):
    states_dev, planes, width_y, width_z = start_block.shape
    cell_total = planes * lax.axis_size("grid") * width_y * width_z
    offset = lax.axis_index("band") * states_dev
    live_count = atom_count[0]
    a_list = []
    b_list = []

    def to_cells(block):
        return lax.all_to_all(block, "band", split_axis=1, concat_axis=0, tiled=True)

    def to_states(block):
        return lax.all_to_all(block, "band", split_axis=0, concat_axis=1, tiled=True)

    def summed(matrix):
        return lax.psum(matrix, ("band", "grid"))

    start_cells = to_cells(start_block)
    cell_shape = start_cells.shape
    start_flat = start_cells.reshape(NB, -1)
    factor, inverse = factor_of(
        summed(jnp.dot(start_flat, start_flat.T, precision=HIGHEST) / cell_total)
    )
    current_cells = jnp.dot(inverse, start_flat, precision=HIGHEST)
    previous_cells = to_cells(previous_block).reshape(NB, -1)
    coupling = previous_coupling
    current_local = to_states(current_cells.reshape(cell_shape))
    for iteration in range(STEPS):
        haloed = extended_2(current_local, (("grid", 1),), 6)
        kinetic_part = kinetic_local(haloed, planes)
        extended = haloed[:, 6:].reshape(states_dev, -1)
        terms = projector_terms(extended, atom_cells, atom_proj, atom_strength, live_count)
        terms = terms.reshape(states_dev, planes + 6, width_y, width_z)
        received = from_behind(terms[:, planes:], "grid", 1)
        own_terms = terms[:, :planes].at[:, :6].add(received)
        applied = kinetic_part + potential[None] * current_local + own_terms
        applied_cells = to_cells(applied).reshape(NB, -1)
        correlation = summed(
            jnp.dot(current_cells, applied_cells.T, precision=HIGHEST) / cell_total
        )
        residual_block = (
            applied_cells
            - jnp.dot(correlation.T, current_cells, precision=HIGHEST)
            - jnp.dot(coupling, previous_cells, precision=HIGHEST)
        )
        factor, inverse = factor_of(
            summed(jnp.dot(residual_block, residual_block.T, precision=HIGHEST) / cell_total)
        )
        coupling = factor.T
        a_list.append(lax.dynamic_slice_in_dim(correlation, offset, states_dev, 1))
        b_list.append(lax.dynamic_slice_in_dim(coupling, offset, states_dev, 1))
        previous_cells = current_cells
        current_cells = jnp.dot(inverse, residual_block, precision=HIGHEST)
        current_local = to_states(current_cells.reshape(cell_shape))
    return (jnp.stack(a_list), jnp.stack(b_list), current_local)


def solution(mesh):
    in_specs = (
        P("band", "grid", None, None),
        P("band", "grid", None, None),
        P(),
        P("grid", None, None),
        P("grid", None),
        P("grid", None, None),
        P("grid", None),
        P("grid"),
    )
    out_specs = (P(None, None, "band"), P(None, None, "band"), P("band", "grid", None, None))
    return jax.shard_map(shards, mesh=mesh, in_specs=in_specs, out_specs=out_specs, check_vma=False)
```

profile of v0, /device:TPU:0, one launch (start us, length us, event | category | flops | bytes accessed | tf_op | source)
XLA Modules:
  0.0 424.2 jit_solution(2157985983389813124)
XLA Ops:
  0.6 1.9 copy.51
  2.6 4.3 %all-to-all-start = ((f32[32,8,4,128]{3,2,0,1:T(4,128)}), f32[32,8,4,128]{3,2,0,1:T(4,128)S(1)}, u32[]{:S(2)}, u32[]{:S(2)}) async-start(f32[32,8,4,128]{3,2,0,1:T(4,128)} %copy.51), calls=%async_computation | async-start | bytes 1048576 | tf_op jit(solution)/shard_map/all_to_all | solution.py:96
  7.6 8.1 %all-to-all-done = f32[32,8,4,128]{3,2,0,1:T(4,128)S(1)} async-done(((f32[32,8,4,128]{3,2,0,1:T(4,128)}), f32[32,8,4,128]{3,2,0,1:T(4,128)S(1)}, u32[]{:S(2)}, u32[]{:S(2)}) %all-to-all-start) | async-done | bytes 524320 | tf_op jit(solution)/shard_map/all_to_all | solution.py:96
  16.5 40.0 %psum.35 = f32[64,64]{0,1:T(8,128)S(1)} all-reduce(f32[64,64]{0,1:T(8,128)S(1)} %convolution_multiply_fusion.4), channel_id=1, replica_groups=mesh['band'=2,'grid'=16] {'band','grid'}, use_global_device_ids=true, to_apply=%region_0.0 | all-reduce | flops 4096 | bytes 32768 | tf_op jit(solution)/shard_map/psum | solution.py:102
  56.6 5.8 %cholesky.59 = f32[64,64]{1,0:T(8,128)S(1)} custom-call(f32[64,64]{1,0:T(8,128)S(1)} %fusion.140), custom_call_target="Cholesky" | custom-call | tf_op jit(solution)/shard_map/jit(cholesky)/cholesky | solution.py:72
  63.8 4.9 %custom-call.7 = f32[1,64,64]{1,2,0:T(8,128)S(1)} custom-call(f32[1,64,64]{2,1,0:T(8,128)S(1)} %fusion.134), custom_call_target="InvertDiagBlocksLowerTriangular" | custom-call | tf_op jit(solution)/shard_map/jit(_solve_triangular)/triangular_solve | solution.py:74
  70.7 3.5 all-to-all-start.1
  74.3 7.9 %all-to-all-done.1 = f32[64,4,4,128]{3,2,1,0:T(4,128)S(1)} async-done(((f32[64,4,4,128]{3,2,1,0:T(4,128)}), f32[64,4,4,128]{3,2,1,0:T(4,128)S(1)}, u32[]{:S(2)}, u32[]{:S(2)}) %all-to-all-start.1) | async-done | bytes 524320 | tf_op jit(solution)/shard_map/all_to_all | solution.py:99
  84.5 2.3 collective-permute-done
  87.6 2.4 copy.56
  90.1 4.8 %gather_fusion = f32[1024,32]{1,0:T(8,128)S(1)} fusion(f32[32,7168]{0,1:T(8,128)} %bitcast.150, s32[1024]{0:T(1024)S(1)} %fusion.141), kind=kCustom, calls=%fused_computation.clone | custom fusion | bytes 266240 | tf_op jit(solution)/shard_map/jit(_take)/gather | solution.py:63
  96.3 8.0 %scatter_custom_fusion = f32[32,7168]{0,1:T(8,128)} fusion(s32[1024]{0:T(1024)S(1)} %bitcast.165, f32[1024,32]{1,0:T(8,128)S(1)} %copy.60, f32[]{:T(128)} %constant.127.clone.1), kind=kCustom, calls=%fused_computation.60 | custom fusion | flops 32768 | bytes 917508 | tf_op jit(solution)/shard_map/scatter-add | solution.py:68
  104.3 3.4 fusion.143
  108.9 8.3 %collective-permute-start.2 = (f32[32,6,4,128]{3,0,2,1:T(8,128)}, f32[32,6,4,128]{3,0,2,1:T(8,128)}, u32[]{:S(2)}, u32[]{:S(2)}) collective-permute-start(f32[32,6,4,128]{3,0,2,1:T(8,128)} %copy.92), channel_id=1, source_target_pairs={{0,1},{1,2},{2,3},{3,4},{4,5},{5,6},{6,7},{7,8},{8,9},{9,10},{10,1... | collective-permute-start | bytes 1179656 | tf_op jit(solution)/shard_map/ppermute | solution.py:36
  117.2 2.0 collective-permute-start.1
  120.2 4.2 all-to-all-start.3
  124.4 1.7 slice.410
  126.1 2.6 copy.91
  128.7 1.4 copy.90
  130.1 1.9 add_dynamic-update-slice_fusion.1
  132.0 4.3 %fusion.51 = f32[32,8,4,128]{3,0,2,1:T(8,128)} fusion(f32[32,8,4,128]{3,0,2,1:T(8,128)} %add_dynamic-update-slice_fusion.1, f32[32,8,4,128]{3,0,2,1:T(8,128)S(1)} %bitcast.145, f32[32,6,4,128]{3,0,2,1:T(8,128)} %collective-permute-done.1, f32[32,6,4,128]{3,0,2,1:T(8,128)} %copy-done.3, f32[8,4,128]{2,1,0:T(4,128)S(1)} %copy-done.7), kind=kLoop, calls=%fused_computation.150 | loop fusion | flops 8388608 | bytes 2375680 | tf_op jit(solution)/shard_map/add | solution.py:122
  136.4 3.7 all-to-all-start.2
  141.4 7.5 %all-to-all-done.2 = f32[32,8,4,128]{3,0,2,1:T(8,128)S(1)} async-done(((f32[32,8,4,128]{3,0,2,1:T(8,128)}), f32[32,8,4,128]{3,0,2,1:T(8,128)S(1)}, u32[]{:S(2)}, u32[]{:S(2)}) %all-to-all-start.2) | async-done | bytes 524320 | tf_op jit(solution)/shard_map/all_to_all | solution.py:96
  150.0 38.9 %psum.36 = f32[64,64]{0,1:T(8,128)S(1)} all-reduce(f32[64,64]{0,1:T(8,128)S(1)} %convolution_multiply_fusion.3), channel_id=1, replica_groups=mesh['band'=2,'grid'=16] {'band','grid'}, use_global_device_ids=true, to_apply=%region_4.8 | all-reduce | flops 4096 | bytes 32768 | tf_op jit(solution)/shard_map/psum | solution.py:102
  190.7 39.4 %psum.37 = f32[64,64]{0,1:T(8,128)S(1)} all-reduce(f32[64,64]{0,1:T(8,128)S(1)} %convolution_multiply_fusion.2), channel_id=1, replica_groups=mesh['band'=2,'grid'=16] {'band','grid'}, use_global_device_ids=true, to_apply=%region_5.9 | all-reduce | flops 4096 | bytes 32768 | tf_op jit(solution)/shard_map/psum | solution.py:102
  230.2 5.8 %cholesky.70 = f32[64,64]{1,0:T(8,128)S(1)} custom-call(f32[64,64]{1,0:T(8,128)S(1)} %fusion.138), custom_call_target="Cholesky" | custom-call | tf_op jit(solution)/shard_map/jit(cholesky)/cholesky | solution.py:72
  237.4 4.9 %custom-call.8 = f32[1,64,64]{1,2,0:T(8,128)S(1)} custom-call(f32[1,64,64]{2,1,0:T(8,128)S(1)} %get-tuple-element.32), custom_call_target="InvertDiagBlocksLowerTriangular" | custom-call | tf_op jit(solution)/shard_map/jit(_solve_triangular)/triangular_solve | solution.py:74
  243.5 10.8 %all_to_all.114 = f32[64,4,4,128]{3,2,1,0:T(4,128)S(1)} all-to-all(f32[64,4,4,128]{3,2,1,0:T(4,128)S(1)} %reshape.189), channel_id=1, replica_groups=mesh['band'=2,'grid'=16] {'band'}, dimensions={0} | all-to-all | bytes 1048576 | tf_op jit(solution)/shard_map/all_to_all | solution.py:99
  256.6 2.3 collective-permute-done.3
  259.7 2.4 copy.71
  262.1 4.8 %gather_fusion.1 = f32[1024,32]{1,0:T(8,128)S(1)} fusion(f32[32,7168]{0,1:T(8,128)} %bitcast.149, s32[1024]{0:T(1024)S(1)} %fusion.141), kind=kCustom, calls=%fused_computation.1.clone | custom fusion | bytes 266240 | tf_op jit(solution)/shard_map/jit(_take)/gather | solution.py:63
  268.4 8.0 %scatter_custom_fusion.1 = f32[32,7168]{0,1:T(8,128)} fusion(s32[1024]{0:T(1024)S(1)} %bitcast.166, f32[1024,32]{1,0:T(8,128)S(1)} %copy.74, f32[]{:T(128)} %constant.127.clone.1), kind=kCustom, calls=%fused_computation.58 | custom fusion | flops 32768 | bytes 917508 | tf_op jit(solution)/shard_map/scatter-add | solution.py:68
  276.4 3.3 fusion.142
  280.9 8.4 %collective-permute-start.5 = (f32[32,6,4,128]{3,0,2,1:T(8,128)}, f32[32,6,4,128]{3,0,2,1:T(8,128)}, u32[]{:S(2)}, u32[]{:S(2)}) collective-permute-start(f32[32,6,4,128]{3,0,2,1:T(8,128)} %copy.95), channel_id=1, source_target_pairs={{0,1},{1,2},{2,3},{3,4},{4,5},{5,6},{6,7},{7,8},{8,9},{9,10},{10,1... | collective-permute-start | bytes 1179656 | tf_op jit(solution)/shard_map/ppermute | solution.py:36
  289.3 2.0 collective-permute-start.4
  291.4 1.7 slice.437
  293.1 2.6 copy.94
  295.7 1.4 copy.93
  297.1 2.0 add_dynamic-update-slice_fusion
  299.0 4.5 %fusion.16 = f32[32,8,4,128]{3,0,2,1:T(8,128)} fusion(f32[32,8,4,128]{3,0,2,1:T(8,128)} %add_dynamic-update-slice_fusion, f32[32,8,4,128]{3,0,2,1:T(8,128)S(1)} %bitcast.148, f32[32,6,4,128]{3,0,2,1:T(8,128)} %collective-permute-done.4, f32[32,6,4,128]{3,0,2,1:T(8,128)} %copy-done.4, f32[8,4,128]{2,1,0:T(4,128)S(1)} %copy-done.7), kind=kLoop, calls=%fused_computation.115 | loop fusion | flops 8388608 | bytes 2375680 | tf_op jit(solution)/shard_map/add | solution.py:122
  303.5 3.5 all-to-all-start.5
  307.1 8.5 %all-to-all-done.5 = f32[32,8,4,128]{3,0,2,1:T(8,128)S(1)} async-done(((f32[32,8,4,128]{3,0,2,1:T(8,128)}), f32[32,8,4,128]{3,0,2,1:T(8,128)S(1)}, u32[]{:S(2)}, u32[]{:S(2)}) %all-to-all-start.5) | async-done | bytes 524320 | tf_op jit(solution)/shard_map/all_to_all | solution.py:96
  316.7 39.2 %psum.38 = f32[64,64]{0,1:T(8,128)S(1)} all-reduce(f32[64,64]{0,1:T(8,128)S(1)} %convolution_multiply_fusion.1), channel_id=1, replica_groups=mesh['band'=2,'grid'=16] {'band','grid'}, use_global_device_ids=true, to_apply=%region_7.11 | all-reduce | flops 4096 | bytes 32768 | tf_op jit(solution)/shard_map/psum | solution.py:102
  357.8 40.5 %psum.39 = f32[64,64]{0,1:T(8,128)S(1)} all-reduce(f32[64,64]{0,1:T(8,128)S(1)} %convolution_multiply_fusion), channel_id=1, replica_groups=mesh['band'=2,'grid'=16] {'band','grid'}, use_global_device_ids=true, to_apply=%region_8.12 | all-reduce | flops 4096 | bytes 32768 | tf_op jit(solution)/shard_map/psum | solution.py:102
  398.3 5.8 %cholesky.81 = f32[64,64]{1,0:T(8,128)S(1)} custom-call(f32[64,64]{1,0:T(8,128)S(1)} %fusion.136), custom_call_target="Cholesky" | custom-call | tf_op jit(solution)/shard_map/jit(cholesky)/cholesky | solution.py:72
  405.5 4.9 %custom-call.9 = f32[1,64,64]{1,2,0:T(8,128)S(1)} custom-call(f32[1,64,64]{2,1,0:T(8,128)S(1)} %get-tuple-element.30), custom_call_target="InvertDiagBlocksLowerTriangular" | custom-call | tf_op jit(solution)/shard_map/jit(_solve_triangular)/triangular_solve | solution.py:74
  412.4 3.5 all-to-all-start.6
  417.2 6.2 %all-to-all-done.6 = f32[64,4,4,128]{3,2,1,0:T(4,128)S(1)} async-done(((f32[64,4,4,128]{3,2,1,0:T(4,128)}), f32[64,4,4,128]{3,2,1,0:T(4,128)S(1)}, u32[]{:S(2)}, u32[]{:S(2)}) %all-to-all-start.6) | async-done | bytes 524320 | tf_op jit(solution)/shard_map/all_to_all | solution.py:99
  (100 shorter events, 31.8 us)
Async XLA Ops:
  0.6 188.9 %copy-start = (f32[64,64]{1,0:T(8,128)S(1)}, f32[64,64]{1,0:T(8,128)}, u32[]{:S(2)}) copy-start(f32[64,64]{1,0:T(8,128)} %param.19) | copy-start | bytes 49156
  2.6 71.6 %copy-start.9 = (f32[8,4]{0,1:T(4,128)S(1)}, f32[8,4]{0,1:T(4,128)}, u32[]{:S(2)}) copy-start(f32[8,4]{0,1:T(4,128)} %param.23) | copy-start | bytes 388
  2.6 71.7 %copy-start.8 = (s32[8,128]{1,0:T(8,128)S(1)}, s32[8,128]{1,0:T(8,128)}, u32[]{:S(2)}) copy-start(s32[8,128]{1,0:T(8,128)} %param.21) | copy-start | bytes 12292
  2.6 13.1 %all-to-all-start = ((f32[32,8,4,128]{3,2,0,1:T(4,128)}), f32[32,8,4,128]{3,2,0,1:T(4,128)S(1)}, u32[]{:S(2)}, u32[]{:S(2)}) async-start(f32[32,8,4,128]{3,2,0,1:T(4,128)} %copy.51), calls=%async_computation | async-start | bytes 1048576 | tf_op jit(solution)/shard_map/all_to_all | solution.py:96
  70.7 11.5 %all-to-all-start.1 = ((f32[64,4,4,128]{3,2,1,0:T(4,128)}), f32[64,4,4,128]{3,2,1,0:T(4,128)S(1)}, u32[]{:S(2)}, u32[]{:S(2)}) async-start(f32[64,4,4,128]{3,2,1,0:T(4,128)} %reshape.180), calls=%async_computation.1 | async-start | bytes 1048576 | tf_op jit(solution)/shard_map/all_to_all | solution.py:99
  83.2 3.6 collective-permute-start
  86.8 0.8 copy-start.3
  87.6 7.5 %copy-start.6 = (f32[8,4,128]{2,1,0:T(4,128)S(1)}, f32[8,4,128]{2,1,0:T(4,128)}, u32[]{:S(2)}) copy-start(f32[8,4,128]{2,1,0:T(4,128)} %param.22) | copy-start | bytes 49156
  104.3 14.9 %copy-start.5 = (f32[32,8,4,128]{3,2,1,0:T(4,128)S(1)}, f32[32,8,4,128]{3,2,1,0:T(4,128)}, u32[]{:S(2)}) copy-start(f32[32,8,4,128]{3,2,1,0:T(4,128)} %param.18) | copy-start | bytes 1572868
  108.9 21.2 %collective-permute-start.2 = (f32[32,6,4,128]{3,0,2,1:T(8,128)}, f32[32,6,4,128]{3,0,2,1:T(8,128)}, u32[]{:S(2)}, u32[]{:S(2)}) collective-permute-start(f32[32,6,4,128]{3,0,2,1:T(8,128)} %copy.92), channel_id=1, source_target_pairs={{0,1},{1,2},{2,3},{3,4},{4,5},{5,6},{6,7},{7,8},{8,9},{9,10},{10,1... | collective-permute-start | bytes 1179656 | tf_op jit(solution)/shard_map/ppermute | solution.py:36
  117.2 14.8 %collective-permute-start.1 = (f32[32,6,4,128]{3,0,2,1:T(8,128)}, f32[32,6,4,128]{3,0,2,1:T(8,128)}, u32[]{:S(2)}, u32[]{:S(2)}) collective-permute-start(f32[32,6,4,128]{3,0,2,1:T(8,128)} %get-tuple-element.40), channel_id=1, source_target_pairs={{0,1},{1,2},{2,3},{3,4},{4,5},{5,6},{6,7},{7,8},{8,9},{9,10},{10,1... | collective-permute-start | bytes 1179656 | tf_op jit(solution)/shard_map/ppermute | solution.py:25
  120.2 16.2 %all-to-all-start.3 = ((f32[32,8,4,128]{3,2,0,1:T(4,128)}), f32[32,8,4,128]{3,2,0,1:T(4,128)}, u32[]{:S(2)}, u32[]{:S(2)}) async-start(f32[32,8,4,128]{3,2,0,1:T(4,128)} %copy.66), calls=%async_computation.3 | async-start | bytes 1048576 | tf_op jit(solution)/shard_map/all_to_all | solution.py:96
  126.1 5.9 %copy-start.7 = (f32[8,4,128]{2,1,0:T(4,128)S(1)}, f32[8,4,128]{2,1,0:T(4,128)}, u32[]{:S(2)}) copy-start(f32[8,4,128]{2,1,0:T(4,128)} %param.20) | copy-start | bytes 49156
  136.4 12.5 %all-to-all-start.2 = ((f32[32,8,4,128]{3,0,2,1:T(8,128)}), f32[32,8,4,128]{3,0,2,1:T(8,128)S(1)}, u32[]{:S(2)}, u32[]{:S(2)}) async-start(f32[32,8,4,128]{3,0,2,1:T(8,128)} %fusion.51), calls=%async_computation.2 | async-start | bytes 1048576 | tf_op jit(solution)/shard_map/all_to_all | solution.py:96
  243.1 11.1 %copy-start.1 = (f32[64,2048]{1,0:T(8,128)}, f32[64,2048]{1,0:T(8,128)S(1)}, u32[]{:S(2)}) copy-start(f32[64,2048]{1,0:T(8,128)S(1)} %fusion.147) | copy-start | bytes 1572868
  255.3 3.6 collective-permute-start.3
  258.9 0.7 copy-start.4
  280.9 16.2 %collective-permute-start.5 = (f32[32,6,4,128]{3,0,2,1:T(8,128)}, f32[32,6,4,128]{3,0,2,1:T(8,128)}, u32[]{:S(2)}, u32[]{:S(2)}) collective-permute-start(f32[32,6,4,128]{3,0,2,1:T(8,128)} %copy.95), channel_id=1, source_target_pairs={{0,1},{1,2},{2,3},{3,4},{4,5},{5,6},{6,7},{7,8},{8,9},{9,10},{10,1... | collective-permute-start | bytes 1179656 | tf_op jit(solution)/shard_map/ppermute | solution.py:36
  289.3 9.7 %collective-permute-start.4 = (f32[32,6,4,128]{3,0,2,1:T(8,128)}, f32[32,6,4,128]{3,0,2,1:T(8,128)}, u32[]{:S(2)}, u32[]{:S(2)}) collective-permute-start(f32[32,6,4,128]{3,0,2,1:T(8,128)} %get-tuple-element.38), channel_id=1, source_target_pairs={{0,1},{1,2},{2,3},{3,4},{4,5},{5,6},{6,7},{7,8},{8,9},{9,10},{10,1... | collective-permute-start | bytes 1179656 | tf_op jit(solution)/shard_map/ppermute | solution.py:25
  297.1 19.1 %copy-start.2 = (f32[64,2048]{1,0:T(8,128)S(1)}, f32[64,2048]{1,0:T(8,128)}, u32[]{:S(2)}) copy-start(f32[64,2048]{1,0:T(8,128)} %copy-done.1) | copy-start | bytes 1572868
  303.5 12.0 %all-to-all-start.5 = ((f32[32,8,4,128]{3,0,2,1:T(8,128)}), f32[32,8,4,128]{3,0,2,1:T(8,128)S(1)}, u32[]{:S(2)}, u32[]{:S(2)}) async-start(f32[32,8,4,128]{3,0,2,1:T(8,128)} %fusion.16), calls=%async_computation.5 | async-start | bytes 1048576 | tf_op jit(solution)/shard_map/all_to_all | solution.py:96
  412.4 11.0 %all-to-all-start.6 = ((f32[64,4,4,128]{3,2,1,0:T(4,128)}), f32[64,4,4,128]{3,2,1,0:T(4,128)S(1)}, u32[]{:S(2)}, u32[]{:S(2)}) async-start(f32[64,4,4,128]{3,2,1,0:T(4,128)} %reshape.195), calls=%async_computation.6 | async-start | bytes 1048576 | tf_op jit(solution)/shard_map/all_to_all | solution.py:99
where the time goes:
time: 426 us; the launch traced here: 424 us
  blocking collectives  209 us (49%)
  other arithmetic  66.8 us (16%)
  local copies, waits for them, and re-layouts  48.4 us (11%)
  starting transfers between devices  46.1 us (11%)
  waiting for transfers between devices  42.7 us (10%)
  matrix products  9.6 us (2%)
    psum x5, blocking collectives, summed(): return lax.psum(matrix, ('band', 'grid'))  198 us
    all_to_all x4, waiting for transfers between devices, to_cells(): lax.all_to_all(block, 'band', split_axis=1, concat_axis=0, tiled=True)  24 us
    another operation x9, other arithmetic, factor_of(): factor = jnp.linalg.cholesky(gram)  19.6 us
    ppermute x2, starting transfers between devices, from_behind(): return lax.ppermute(block, axis, route)  16.7 us
    another operation x6, other arithmetic, factor_of(): inverse = jax.scipy.linalg.solve_triangular(factor, identity, lower=True)  16.6 us
    scatter-add x2, other arithmetic, projector_terms(): jnp.zeros_like(extended).at[:, cell_list]  16 us
    all_to_all x4, starting transfers between devices, to_cells(): lax.all_to_all(block, 'band', split_axis=1, concat_axis=0, tiled=True)  15.7 us
    unnamed x28, local copies, waits for them, and re-layouts  14.7 us
  transfers between devices with their start and end apart: 12, of which 7 were waited for; matrix products, arithmetic and copies ran while one was open for 5% of the time, Pallas kernels for 0%

commit v1 on v0

--- a/solution.py
+++ b/solution.py
@@ -14,6 +14,15 @@
     -1.0 / 112.0,
     2.0 / 1925.0,
     -1.0 / 16632.0,
+)
+detail_ways = lambda my_tile, lane_axis: jnp.concatenate(
+    lax.all_to_all(
+        jnp.stack(jnp.split(my_tile, lax.psum(1, axis_name=lane_axis), 0), 0),
+        axis_name=lane_axis,
+        split_axis=0,
+        concat_axis=0,
+    ),
+    1,
 )
 
 
@@ -96,7 +105,7 @@
         return lax.all_to_all(block, "band", split_axis=1, concat_axis=0, tiled=True)
 
     def to_states(block):
-        return lax.all_to_all(block, "band", split_axis=0, concat_axis=1, tiled=True)
+        return detail_ways(block, "band")
 
     def summed(matrix):
         return lax.psum(matrix, ("band", "grid"))

time: 426 us -> 427 us (level)
  no operation moved by 1% of the time
where the time goes in v1:
time: 427 us; the launch traced here: 425 us
  blocking collectives  209 us (49%)
  other arithmetic  68.6 us (16%)
  local copies, waits for them, and re-layouts  47.8 us (11%)
  starting transfers between devices  45.8 us (11%)
  waiting for transfers between devices  42.8 us (10%)
  matrix products  9.61 us (2%)
    psum x5, blocking collectives, summed(): return lax.psum(matrix, ('band', 'grid'))  198 us
    all_to_all x4, waiting for transfers between devices, to_cells(): lax.all_to_all(block, 'band', split_axis=1, concat_axis=0, tiled=True)  24 us
    another operation x9, other arithmetic, factor_of(): factor = jnp.linalg.cholesky(gram)  19.6 us
    another operation x6, other arithmetic, factor_of(): inverse = jax.scipy.linalg.solve_triangular(factor, identity, lower=True)  16.6 us
    ppermute x2, starting transfers between devices, from_behind(): return lax.ppermute(block, axis, route)  16.5 us
    scatter-add x2, other arithmetic, projector_terms(): jnp.zeros_like(extended).at[:, cell_list]  16 us
    all_to_all x4, starting transfers between devices, to_cells(): lax.all_to_all(block, 'band', split_axis=1, concat_axis=0, tiled=True)  15.6 us
    unnamed x28, local copies, waits for them, and re-layouts  15.5 us
  transfers between devices with their start and end apart: 12, of which 7 were waited for; matrix products, arithmetic and copies ran while one was open for 5% of the time, Pallas kernels for 0%

profile of v1, /device:TPU:0, one launch (start us, length us, event | category | flops | bytes accessed | tf_op | source)
XLA Modules:
  0.0 425.2 jit_solution(3593759279724108662)
XLA Ops:
  0.6 1.9 copy.51
  2.6 4.2 all-to-all-start
  7.4 8.1 %all-to-all-done = f32[32,8,4,128]{3,2,0,1:T(4,128)S(1)} async-done(((f32[32,8,4,128]{3,2,0,1:T(4,128)}), f32[32,8,4,128]{3,2,0,1:T(4,128)S(1)}, u32[]{:S(2)}, u32[]{:S(2)}) %all-to-all-start) | async-done | bytes 524320 | tf_op jit(solution)/shard_map/all_to_all | solution.py:105
  16.4 40.0 %psum.35 = f32[64,64]{0,1:T(8,128)S(1)} all-reduce(f32[64,64]{0,1:T(8,128)S(1)} %convolution_multiply_fusion.4), channel_id=1, replica_groups=mesh['band'=2,'grid'=16] {'band','grid'}, use_global_device_ids=true, to_apply=%region_0.0 | all-reduce | flops 4096 | bytes 32768 | tf_op jit(solution)/shard_map/psum | solution.py:111
  56.5 5.8 %cholesky.59 = f32[64,64]{1,0:T(8,128)S(1)} custom-call(f32[64,64]{1,0:T(8,128)S(1)} %fusion.140), custom_call_target="Cholesky" | custom-call | tf_op jit(solution)/shard_map/jit(cholesky)/cholesky | solution.py:81
  63.7 4.9 %custom-call.7 = f32[1,64,64]{1,2,0:T(8,128)S(1)} custom-call(f32[1,64,64]{2,1,0:T(8,128)S(1)} %fusion.134), custom_call_target="InvertDiagBlocksLowerTriangular" | custom-call | tf_op jit(solution)/shard_map/jit(_solve_triangular)/triangular_solve | solution.py:83
  70.9 3.5 all-to-all-start.1
  74.5 7.9 %all-to-all-done.1 = f32[2,32,4,4,128]{4,1,3,2,0:T(8,128)S(1)} async-done(((f32[2,32,4,4,128]{4,1,3,2,0:T(8,128)}), f32[2,32,4,4,128]{4,1,3,2,0:T(8,128)S(1)}, u32[]{:S(2)}, u32[]{:S(2)}) %all-to-all-start.1) | async-done | bytes 524320 | tf_op jit(solution)/shard_map/all_to_all | solution.py:19
  84.5 2.3 collective-permute-done
  87.7 2.4 copy.57
  90.1 4.8 %gather_fusion = f32[1024,32]{1,0:T(8,128)S(1)} fusion(f32[32,7168]{0,1:T(8,128)} %bitcast.146, s32[1024]{0:T(1024)S(1)} %fusion.141), kind=kCustom, calls=%fused_computation.clone | custom fusion | bytes 266240 | tf_op jit(solution)/shard_map/jit(_take)/gather | solution.py:72
  96.3 8.0 %scatter_custom_fusion = f32[32,7168]{0,1:T(8,128)} fusion(s32[1024]{0:T(1024)S(1)} %bitcast.159, f32[1024,32]{1,0:T(8,128)S(1)} %copy.61, f32[]{:T(128)} %constant.127.clone.1), kind=kCustom, calls=%fused_computation.60 | custom fusion | flops 32768 | bytes 917508 | tf_op jit(solution)/shard_map/scatter-add | solution.py:77
  104.4 3.4 fusion.143
  108.9 8.3 %collective-permute-start.2 = (f32[32,6,4,128]{3,0,2,1:T(8,128)}, f32[32,6,4,128]{3,0,2,1:T(8,128)}, u32[]{:S(2)}, u32[]{:S(2)}) collective-permute-start(f32[32,6,4,128]{3,0,2,1:T(8,128)} %copy.94), channel_id=1, source_target_pairs={{0,1},{1,2},{2,3},{3,4},{4,5},{5,6},{6,7},{7,8},{8,9},{9,10},{10,1... | collective-permute-start | bytes 1179656 | tf_op jit(solution)/shard_map/ppermute | solution.py:45
  117.3 2.0 collective-permute-start.1
  120.2 4.2 all-to-all-start.3
  124.4 1.7 slice.416
  126.2 2.6 copy.93
  128.8 1.4 copy.92
  130.1 1.9 add_dynamic-update-slice_fusion.1
  132.1 4.3 %fusion.51 = f32[32,8,4,128]{3,0,2,1:T(8,128)} fusion(f32[32,8,4,128]{3,0,2,1:T(8,128)} %add_dynamic-update-slice_fusion.1, f32[32,8,4,128]{3,0,2,1:T(8,128)S(1)} %bitcast.141, f32[32,6,4,128]{3,0,2,1:T(8,128)} %collective-permute-done.1, f32[32,6,4,128]{3,0,2,1:T(8,128)} %copy-done.3, f32[8,4,128]{2,1,0:T(4,128)S(1)} %copy-done.7), kind=kLoop, calls=%fused_computation.150 | loop fusion | flops 8388608 | bytes 2375680 | tf_op jit(solution)/shard_map/add | solution.py:131
  136.4 3.7 all-to-all-start.2
  141.5 7.5 %all-to-all-done.2 = f32[32,8,4,128]{3,0,2,1:T(8,128)S(1)} async-done(((f32[32,8,4,128]{3,0,2,1:T(8,128)}), f32[32,8,4,128]{3,0,2,1:T(8,128)S(1)}, u32[]{:S(2)}, u32[]{:S(2)}) %all-to-all-start.2) | async-done | bytes 524320 | tf_op jit(solution)/shard_map/all_to_all | solution.py:105
  150.1 39.0 %psum.36 = f32[64,64]{0,1:T(8,128)S(1)} all-reduce(f32[64,64]{0,1:T(8,128)S(1)} %convolution_multiply_fusion.3), channel_id=1, replica_groups=mesh['band'=2,'grid'=16] {'band','grid'}, use_global_device_ids=true, to_apply=%region_4.8 | all-reduce | flops 4096 | bytes 32768 | tf_op jit(solution)/shard_map/psum | solution.py:111
  190.8 39.3 %psum.37 = f32[64,64]{0,1:T(8,128)S(1)} all-reduce(f32[64,64]{0,1:T(8,128)S(1)} %convolution_multiply_fusion.2), channel_id=1, replica_groups=mesh['band'=2,'grid'=16] {'band','grid'}, use_global_device_ids=true, to_apply=%region_5.9 | all-reduce | flops 4096 | bytes 32768 | tf_op jit(solution)/shard_map/psum | solution.py:111
  230.2 5.8 %cholesky.70 = f32[64,64]{1,0:T(8,128)S(1)} custom-call(f32[64,64]{1,0:T(8,128)S(1)} %fusion.138), custom_call_target="Cholesky" | custom-call | tf_op jit(solution)/shard_map/jit(cholesky)/cholesky | solution.py:81
  237.4 4.9 %custom-call.8 = f32[1,64,64]{1,2,0:T(8,128)S(1)} custom-call(f32[1,64,64]{2,1,0:T(8,128)S(1)} %get-tuple-element.32), custom_call_target="InvertDiagBlocksLowerTriangular" | custom-call | tf_op jit(solution)/shard_map/jit(_solve_triangular)/triangular_solve | solution.py:83
  244.6 10.8 %all_to_all.75 = f32[2,32,4,4,128]{4,1,3,2,0:T(8,128)S(1)} all-to-all(f32[2,32,4,4,128]{4,1,3,2,0:T(8,128)S(1)} %pad_maximum_fusion.5), channel_id=1, replica_groups=mesh['band'=2,'grid'=16] {'band'}, dimensions={0} | all-to-all | bytes 1048576 | tf_op jit(solution)/shard_map/all_to_all | solution.py:19
  257.5 2.3 collective-permute-done.3
  260.6 2.4 copy.73
  263.1 4.8 %gather_fusion.1 = f32[1024,32]{1,0:T(8,128)S(1)} fusion(f32[32,7168]{0,1:T(8,128)} %bitcast.145, s32[1024]{0:T(1024)S(1)} %fusion.141), kind=kCustom, calls=%fused_computation.1.clone | custom fusion | bytes 266240 | tf_op jit(solution)/shard_map/jit(_take)/gather | solution.py:72
  269.3 8.0 %scatter_custom_fusion.1 = f32[32,7168]{0,1:T(8,128)} fusion(s32[1024]{0:T(1024)S(1)} %bitcast.160, f32[1024,32]{1,0:T(8,128)S(1)} %copy.76, f32[]{:T(128)} %constant.127.clone.1), kind=kCustom, calls=%fused_computation.58 | custom fusion | flops 32768 | bytes 917508 | tf_op jit(solution)/shard_map/scatter-add | solution.py:77
  277.3 3.3 fusion.142
  281.9 8.2 %collective-permute-start.5 = (f32[32,6,4,128]{3,0,2,1:T(8,128)}, f32[32,6,4,128]{3,0,2,1:T(8,128)}, u32[]{:S(2)}, u32[]{:S(2)}) collective-permute-start(f32[32,6,4,128]{3,0,2,1:T(8,128)} %copy.97), channel_id=1, source_target_pairs={{0,1},{1,2},{2,3},{3,4},{4,5},{5,6},{6,7},{7,8},{8,9},{9,10},{10,1... | collective-permute-start | bytes 1179656 | tf_op jit(solution)/shard_map/ppermute | solution.py:45
  290.0 2.0 collective-permute-start.4
  292.1 1.7 slice.443
  293.8 2.6 copy.96
  296.4 1.4 copy.95
  297.8 2.0 add_dynamic-update-slice_fusion
  299.8 4.5 %fusion.16 = f32[32,8,4,128]{3,0,2,1:T(8,128)} fusion(f32[32,8,4,128]{3,0,2,1:T(8,128)} %add_dynamic-update-slice_fusion, f32[32,8,4,128]{3,0,2,1:T(8,128)S(1)} %bitcast.144, f32[32,6,4,128]{3,0,2,1:T(8,128)} %collective-permute-done.4, f32[32,6,4,128]{3,0,2,1:T(8,128)} %copy-done.4, f32[8,4,128]{2,1,0:T(4,128)S(1)} %copy-done.7), kind=kLoop, calls=%fused_computation.115 | loop fusion | flops 8388608 | bytes 2375680 | tf_op jit(solution)/shard_map/add | solution.py:131
  304.3 3.5 all-to-all-start.5
  307.8 8.5 %all-to-all-done.5 = f32[32,8,4,128]{3,0,2,1:T(8,128)S(1)} async-done(((f32[32,8,4,128]{3,0,2,1:T(8,128)}), f32[32,8,4,128]{3,0,2,1:T(8,128)S(1)}, u32[]{:S(2)}, u32[]{:S(2)}) %all-to-all-start.5) | async-done | bytes 524320 | tf_op jit(solution)/shard_map/all_to_all | solution.py:105
  317.4 39.3 %psum.38 = f32[64,64]{0,1:T(8,128)S(1)} all-reduce(f32[64,64]{0,1:T(8,128)S(1)} %convolution_multiply_fusion.1), channel_id=1, replica_groups=mesh['band'=2,'grid'=16] {'band','grid'}, use_global_device_ids=true, to_apply=%region_7.11 | all-reduce | flops 4096 | bytes 32768 | tf_op jit(solution)/shard_map/psum | solution.py:111
  358.6 40.4 %psum.39 = f32[64,64]{0,1:T(8,128)S(1)} all-reduce(f32[64,64]{0,1:T(8,128)S(1)} %convolution_multiply_fusion), channel_id=1, replica_groups=mesh['band'=2,'grid'=16] {'band','grid'}, use_global_device_ids=true, to_apply=%region_8.12 | all-reduce | flops 4096 | bytes 32768 | tf_op jit(solution)/shard_map/psum | solution.py:111
  399.1 5.8 %cholesky.81 = f32[64,64]{1,0:T(8,128)S(1)} custom-call(f32[64,64]{1,0:T(8,128)S(1)} %fusion.136), custom_call_target="Cholesky" | custom-call | tf_op jit(solution)/shard_map/jit(cholesky)/cholesky | solution.py:81
  406.3 4.9 %custom-call.9 = f32[1,64,64]{1,2,0:T(8,128)S(1)} custom-call(f32[1,64,64]{2,1,0:T(8,128)S(1)} %get-tuple-element.30), custom_call_target="InvertDiagBlocksLowerTriangular" | custom-call | tf_op jit(solution)/shard_map/jit(_solve_triangular)/triangular_solve | solution.py:83
  413.3 3.5 all-to-all-start.6
  418.1 6.2 %all-to-all-done.6 = f32[2,32,4,4,128]{4,3,2,1,0:T(4,128)S(1)} async-done(((f32[2,32,4,4,128]{4,3,2,1,0:T(4,128)}), f32[2,32,4,4,128]{4,3,2,1,0:T(4,128)S(1)}, u32[]{:S(2)}, u32[]{:S(2)}) %all-to-all-start.6) | async-done | bytes 524320 | tf_op jit(solution)/shard_map/all_to_all | solution.py:19
  (111 shorter events, 33.0 us)
Async XLA Ops:
  0.6 189.0 %copy-start = (f32[64,64]{1,0:T(8,128)S(1)}, f32[64,64]{1,0:T(8,128)}, u32[]{:S(2)}) copy-start(f32[64,64]{1,0:T(8,128)} %param.19) | copy-start | bytes 49156
  2.6 12.9 %all-to-all-start = ((f32[32,8,4,128]{3,2,0,1:T(4,128)}), f32[32,8,4,128]{3,2,0,1:T(4,128)S(1)}, u32[]{:S(2)}, u32[]{:S(2)}) async-start(f32[32,8,4,128]{3,2,0,1:T(4,128)} %copy.51), calls=%async_computation | async-start | bytes 1048576 | tf_op jit(solution)/shard_map/all_to_all | solution.py:105
  15.8 58.6 %copy-start.9 = (f32[8,4]{0,1:T(4,128)S(1)}, f32[8,4]{0,1:T(4,128)}, u32[]{:S(2)}) copy-start(f32[8,4]{0,1:T(4,128)} %param.23) | copy-start | bytes 388
  15.8 58.6 %copy-start.8 = (s32[8,128]{1,0:T(8,128)S(1)}, s32[8,128]{1,0:T(8,128)}, u32[]{:S(2)}) copy-start(s32[8,128]{1,0:T(8,128)} %param.21) | copy-start | bytes 12292
  70.9 11.5 %all-to-all-start.1 = ((f32[2,32,4,4,128]{4,1,3,2,0:T(8,128)}), f32[2,32,4,4,128]{4,1,3,2,0:T(8,128)S(1)}, u32[]{:S(2)}, u32[]{:S(2)}) async-start(f32[2,32,4,4,128]{4,1,3,2,0:T(8,128)} %pad_maximum_fusion.4), calls=%async_computation.1 | async-start | bytes 1048576 | tf_op jit(solution)/shard_map/all_to_all | solution.py:19
  83.2 3.6 collective-permute-start
  86.8 0.8 copy-start.3
  87.6 7.5 %copy-start.6 = (f32[8,4,128]{2,1,0:T(4,128)S(1)}, f32[8,4,128]{2,1,0:T(4,128)}, u32[]{:S(2)}) copy-start(f32[8,4,128]{2,1,0:T(4,128)} %param.22) | copy-start | bytes 49156
  104.4 14.9 %copy-start.5 = (f32[32,8,4,128]{3,2,1,0:T(4,128)S(1)}, f32[32,8,4,128]{3,2,1,0:T(4,128)}, u32[]{:S(2)}) copy-start(f32[32,8,4,128]{3,2,1,0:T(4,128)} %param.18) | copy-start | bytes 1572868
  108.9 21.2 %collective-permute-start.2 = (f32[32,6,4,128]{3,0,2,1:T(8,128)}, f32[32,6,4,128]{3,0,2,1:T(8,128)}, u32[]{:S(2)}, u32[]{:S(2)}) collective-permute-start(f32[32,6,4,128]{3,0,2,1:T(8,128)} %copy.94), channel_id=1, source_target_pairs={{0,1},{1,2},{2,3},{3,4},{4,5},{5,6},{6,7},{7,8},{8,9},{9,10},{10,1... | collective-permute-start | bytes 1179656 | tf_op jit(solution)/shard_map/ppermute | solution.py:45
  117.3 14.8 %collective-permute-start.1 = (f32[32,6,4,128]{3,0,2,1:T(8,128)}, f32[32,6,4,128]{3,0,2,1:T(8,128)}, u32[]{:S(2)}, u32[]{:S(2)}) collective-permute-start(f32[32,6,4,128]{3,0,2,1:T(8,128)} %get-tuple-element.44), channel_id=1, source_target_pairs={{0,1},{1,2},{2,3},{3,4},{4,5},{5,6},{6,7},{7,8},{8,9},{9,10},{10,1... | collective-permute-start | bytes 1179656 | tf_op jit(solution)/shard_map/ppermute | solution.py:34
  120.2 16.2 %all-to-all-start.3 = ((f32[32,8,4,128]{3,2,0,1:T(4,128)}), f32[32,8,4,128]{3,2,0,1:T(4,128)}, u32[]{:S(2)}, u32[]{:S(2)}) async-start(f32[32,8,4,128]{3,2,0,1:T(4,128)} %copy.67), calls=%async_computation.3 | async-start | bytes 1048576 | tf_op jit(solution)/shard_map/all_to_all | solution.py:105
  126.2 5.9 %copy-start.7 = (f32[8,4,128]{2,1,0:T(4,128)S(1)}, f32[8,4,128]{2,1,0:T(4,128)}, u32[]{:S(2)}) copy-start(f32[8,4,128]{2,1,0:T(4,128)} %param.20) | copy-start | bytes 49156
  136.4 12.5 %all-to-all-start.2 = ((f32[32,8,4,128]{3,0,2,1:T(8,128)}), f32[32,8,4,128]{3,0,2,1:T(8,128)S(1)}, u32[]{:S(2)}, u32[]{:S(2)}) async-start(f32[32,8,4,128]{3,0,2,1:T(8,128)} %fusion.51), calls=%async_computation.2 | async-start | bytes 1048576 | tf_op jit(solution)/shard_map/all_to_all | solution.py:105
  243.2 0.8 copy-start.1
  256.2 3.6 collective-permute-start.3
  259.8 0.7 copy-start.4
  281.9 15.9 %collective-permute-start.5 = (f32[32,6,4,128]{3,0,2,1:T(8,128)}, f32[32,6,4,128]{3,0,2,1:T(8,128)}, u32[]{:S(2)}, u32[]{:S(2)}) collective-permute-start(f32[32,6,4,128]{3,0,2,1:T(8,128)} %copy.97), channel_id=1, source_target_pairs={{0,1},{1,2},{2,3},{3,4},{4,5},{5,6},{6,7},{7,8},{8,9},{9,10},{10,1... | collective-permute-start | bytes 1179656 | tf_op jit(solution)/shard_map/ppermute | solution.py:45
  290.0 9.7 %collective-permute-start.4 = (f32[32,6,4,128]{3,0,2,1:T(8,128)}, f32[32,6,4,128]{3,0,2,1:T(8,128)}, u32[]{:S(2)}, u32[]{:S(2)}) collective-permute-start(f32[32,6,4,128]{3,0,2,1:T(8,128)} %get-tuple-element.40), channel_id=1, source_target_pairs={{0,1},{1,2},{2,3},{3,4},{4,5},{5,6},{6,7},{7,8},{8,9},{9,10},{10,1... | collective-permute-start | bytes 1179656 | tf_op jit(solution)/shard_map/ppermute | solution.py:34
  297.8 19.1 %copy-start.2 = (f32[64,2048]{1,0:T(8,128)S(1)}, f32[64,2048]{1,0:T(8,128)}, u32[]{:S(2)}) copy-start(f32[64,2048]{1,0:T(8,128)} %copy-done.1) | copy-start | bytes 1572868
  304.3 12.0 %all-to-all-start.5 = ((f32[32,8,4,128]{3,0,2,1:T(8,128)}), f32[32,8,4,128]{3,0,2,1:T(8,128)S(1)}, u32[]{:S(2)}, u32[]{:S(2)}) async-start(f32[32,8,4,128]{3,0,2,1:T(8,128)} %fusion.16), calls=%async_computation.5 | async-start | bytes 1048576 | tf_op jit(solution)/shard_map/all_to_all | solution.py:105
  413.3 11.0 %all-to-all-start.6 = ((f32[2,32,4,4,128]{4,3,2,1,0:T(4,128)}), f32[2,32,4,4,128]{4,3,2,1,0:T(4,128)S(1)}, u32[]{:S(2)}, u32[]{:S(2)}) async-start(f32[2,32,4,4,128]{4,3,2,1,0:T(4,128)} %pad_maximum_fusion.6), calls=%async_computation.6 | async-start | bytes 1048576 | tf_op jit(solution)/shard_map/all_to_all | solution.py:19
